TPU v7x, 256 devices: a whole 4x4x8 slice. The times are simulated.
256 devices in a mesh: branch: 64 (over z, y, x_lo), rows: 4 (over x_hi, core).
Axes of the slice: x: 4 (x_hi: 2, x_lo: 2; x = x_hi * 2 + x_lo), y: 4, z: 8, core: 2. Of those that a mesh axis runs over, the one named last changes fastest.
Arguments:
- points: float32 [3, 524288], P(None, ('branch', 'rows')), may hold values from 0 to 1, as said below
- noise: float32 [524288], P(('branch', 'rows')), may hold values from 0.2 to 2
- landmarks: float32 [7, 3, 256], replicated, may hold values from 0 to 1, as said below
- mixing: float32 [7, 256, 256], replicated, may hold values from -6 to 6
Outputs:
- bases: float32 [3, 524288, 256], P(None, ('branch', 'rows'))
- factors: float32 [64, 3, 256, 256], P('branch')
Inputs may be any that keep to these rules, and one draw needn't show every extreme that they name: `points`: coordinates lie in the unit cube. `landmarks`: coordinates lie in the unit cube.
All inputs are finite; a program needn't handle non-finite values.
Results may differ from a plain program's by a relative error of at most 0.00025.
Values sent between devices are 32-bit elements; how exact they have to be, the bound alone decides.
A program may use at most 128 MiB of HBM per device.

v0:
```python
import jax
import jax.numpy as jnp
from jax import lax
from jax.sharding import PartitionSpec as P

highest = lax.Precision.HIGHEST


def partner(value, axis, bit):
    return lax.ppermute(value, axis, [(i, i ^ 1 << bit) for i in range(lax.axis_size(axis))])


def kernel_block(positions, landmark_set, length_scale):
    spread = jnp.zeros((positions.shape[1], landmark_set.shape[1]), jnp.float32)
    for component in range(3):
        offset = positions[component][:, None] - landmark_set[component][None, :]
        spread = spread + offset * offset
    return jnp.exp(-spread / (2.0 * length_scale * length_scale))


def project(left, right):
    return jnp.einsum(
        "nr,ns->rs", left, right, precision=highest, preferred_element_type=jnp.float32
    )


def solve_with(factor, right_side):
    return jax.scipy.linalg.cho_solve((factor, True), right_side)


def group_total(partial_value, width_bits):
    summed = lax.psum(partial_value, "rows")
    for bit_index in range(width_bits):
        summed = summed + partner(summed, "branch", bit_index)
    return summed


def on_device(points, noise, landmarks, mixing):
    width_rank = mixing.shape[1]
    local_rows = points.shape[1]
    branch_bits = lax.axis_size("branch").bit_length() - 1
    row_devices = lax.axis_size("rows")
    length_scale = 0.6 * width_rank ** (-1.0 / 3.0)
    position = lax.axis_index("branch")
    identity = jnp.eye(width_rank, dtype=jnp.float32)
    unit_list = []
    node_bits = []
    node_rows = []
    for level_index in range(3):
        width_bits = branch_bits - 2 + level_index
        node_id = 2 ** (2 - level_index) - 1 + position // 2**width_bits
        landmark_set = lax.dynamic_index_in_dim(landmarks, node_id, 0, keepdims=False)
        mixing_now = lax.dynamic_index_in_dim(mixing, node_id, 0, keepdims=False)
        kernel = kernel_block(points, landmark_set, length_scale)
        unit_list.append(
            jnp.dot(kernel, mixing_now, precision=highest, preferred_element_type=jnp.float32)
        )
        node_bits.append(width_bits)
        node_rows.append(float(2**width_bits * row_devices * local_rows))
    bases = []
    factor_list = []
    coefficients = {}
    for level_index in range(3):
        for prior_index in range(level_index):
            cross = group_total(
                project(bases[prior_index], unit_list[level_index]), node_bits[prior_index]
            )
            coefficients[prior_index, level_index] = (
                solve_with(factor_list[prior_index], cross) / node_rows[prior_index]
            )
        current = unit_list[level_index] / noise[:, None]
        for prior_index in range(level_index):
            current = current - jnp.dot(
                bases[prior_index],
                coefficients[prior_index, level_index],
                precision=highest,
                preferred_element_type=jnp.float32,
            )
        bases.append(current)
        gram_matrix = group_total(project(current, unit_list[level_index]), node_bits[level_index])
        factor = jnp.linalg.cholesky(identity + gram_matrix / node_rows[level_index])
        factor_list.append(factor)
    return (jnp.stack(bases, axis=0), jnp.stack(factor_list, axis=0)[None])


def solution(mesh):
    in_specs = (P(None, ("branch", "rows")), P(("branch", "rows")), P(), P())
    out_specs = (P(None, ("branch", "rows"), None), P("branch", None, None, None))
    return jax.shard_map(
        on_device, mesh=mesh, in_specs=in_specs, out_specs=out_specs, check_vma=False
    )
```

profile of v0, /device:TPU:8, one launch (start us, length us, event | category | flops | bytes accessed | tf_op | source)
XLA Modules:
  0.0 528.9 jit_solution(15413675945931273060)
XLA Ops:
  9.1 2.5 fusion.24
  11.6 4.7 fusion.127
  20.1 5.1 fusion.126
  25.2 50.5 %all-reduce.11.cloned.1.call-done = (f32[256,256]{0,1:T(8,128)}, f32[256,256]{1,0:T(8,128)}) async-done(((f32[256,256]{0,1:T(8,128)}, f32[256,256]{1,0:T(8,128)}), (f32[256,256]{0,1:T(8,128)}, f32[256,256]{1,0:T(8,128)})) %all-reduce.11.cloned.1.call-update) | async-done | bytes 524304 | tf_op jit(solution)/shard_map/psum | solution.py:32
  77.7 7.4 %collective-permute-done = f32[256,256]{0,1:T(8,128)S(1)} collective-permute-done((f32[256,256]{0,1:T(8,128)}, f32[256,256]{0,1:T(8,128)S(1)}, u32[]{:S(2)}, u32[]{:S(2)}) %collective-permute-start) | collective-permute-done | bytes 262176 | tf_op jit(solution)/shard_map/ppermute | solution.py:10
  86.7 3.4 collective-permute-done.4
  102.6 4.3 collective-permute-done.2
  108.6 4.6 fusion.125
  114.2 11.7 %cholesky.172 = f32[128,128]{1,0:T(8,128)S(1)} custom-call(f32[128,128]{1,0:T(8,128)S(1)} %cholesky.270), custom_call_target="Cholesky" | custom-call | tf_op jit(solution)/shard_map/jit(cholesky)/cholesky | solution.py:81
  126.0 9.8 %custom-call.17 = f32[1,128,128]{1,2,0:T(8,128)S(1)} custom-call(f32[1,128,128]{2,1,0:T(8,128)S(1)} %get-tuple-element.67), custom_call_target="InvertDiagBlocksLowerTriangular" | custom-call | tf_op jit(solution)/shard_map/jit(cholesky)/cholesky | solution.py:81
  136.3 11.7 %cholesky.189 = f32[128,128]{1,0:T(8,128)S(1)} custom-call(f32[128,128]{1,0:T(8,128)S(1)} %convolution_subtract_fusion.8), custom_call_target="Cholesky" | custom-call | tf_op jit(solution)/shard_map/jit(cholesky)/cholesky | solution.py:81
  150.1 4.0 while.6
  154.2 19.9 %custom-call.18 = f32[2,128,128]{1,2,0:T(8,128)S(1)} custom-call(f32[2,128,128]{2,1,0:T(8,128)S(1)} %get-tuple-element.24), custom_call_target="InvertDiagBlocksLowerTriangular" | custom-call | tf_op jit(solution)/shard_map/jit(_cho_solve)/triangular_solve | solution.py:28
  176.1 4.3 convolution_subtract_fusion.2
  180.5 4.3 fusion.132
  184.8 4.3 fusion.133
  189.1 47.9 %all-reduce.9.cloned.1.call-done = (f32[256,256]{1,0:T(8,128)}, f32[256,256]{1,0:T(8,128)}, f32[256,256]{0,1:T(8,128)}) async-done(((f32[256,256]{1,0:T(8,128)}, f32[256,256]{1,0:T(8,128)}, f32[256,256]{0,1:T(8,128)}), (f32[256,256]{1,0:T(8,128)}, f32[256,256]{1,0:T(8,128)}, f32[256,256]{0,1:T(8,128)})) %all-reduce.9.cloned.1.call-update) | async-done | bytes 786448 | tf_op jit(solution)/shard_map/psum | solution.py:32
  239.7 6.8 %collective-permute-done.12 = f32[256,256]{0,1:T(8,128)S(1)} collective-permute-done((f32[256,256]{0,1:T(8,128)}, f32[256,256]{0,1:T(8,128)S(1)}, u32[]{:S(2)}, u32[]{:S(2)}) %collective-permute-start.12) | collective-permute-done | bytes 262176 | tf_op jit(solution)/shard_map/ppermute | solution.py:10
  248.5 3.6 collective-permute-done.8
  253.7 3.4 collective-permute-done.17
  258.8 2.5 collective-permute-start.14
  263.4 4.0 collective-permute-done.18
  269.6 4.3 collective-permute-done.14
  275.6 3.9 collective-permute-done.10
  281.2 2.9 collective-permute-done.19
  285.8 2.6 collective-permute-start.16
  290.8 6.4 %collective-permute-done.20 = f32[256,256]{1,0:T(8,128)S(1)} collective-permute-done((f32[256,256]{1,0:T(8,128)S(1)}, f32[256,256]{1,0:T(8,128)S(1)}, u32[]{:S(2)}, u32[]{:S(2)}) %collective-permute-start.20) | collective-permute-done | bytes 262176 | tf_op jit(solution)/shard_map/ppermute | solution.py:10
  298.4 5.5 %convolution_subtract_fusion.1 = f32[2048,256]{1,0:T(8,128)} fusion(f32[2048,256]{1,0:T(8,128)} %copy-done.5, f32[2048]{0:T(1024)S(1)} %copy-done.13, f32[128,256]{0,1:T(8,128)} %copy.9, f32[128,256]{0,1:T(8,128)S(1)} %fusion.103, f32[2048,256]{1,0:T(8,128)} %copy-done.8), kind=kOutput, calls=%fused_computation.6 | convolution fusion | flops 1612316672 | bytes 6561792 | tf_op jit(solution)/shard_map/dot_general | solution.py:73
  305.1 11.7 %cholesky.206 = f32[128,128]{1,0:T(8,128)S(1)} custom-call(f32[128,128]{1,0:T(8,128)S(1)} %cholesky.273), custom_call_target="Cholesky" | custom-call | tf_op jit(solution)/shard_map/jit(cholesky)/cholesky | solution.py:81
  316.8 9.8 %custom-call.20 = f32[1,128,128]{1,2,0:T(8,128)S(1)} custom-call(f32[1,128,128]{2,1,0:T(8,128)S(1)} %get-tuple-element.63), custom_call_target="InvertDiagBlocksLowerTriangular" | custom-call | tf_op jit(solution)/shard_map/jit(cholesky)/cholesky | solution.py:81
  327.1 12.1 %cholesky.223 = f32[128,128]{1,0:T(8,128)S(1)} custom-call(f32[128,128]{1,0:T(8,128)S(1)} %convolution_subtract_fusion.7), custom_call_target="Cholesky" | custom-call | tf_op jit(solution)/shard_map/jit(cholesky)/cholesky | solution.py:81
  342.0 4.1 while.7
  346.0 19.7 %custom-call.21 = f32[2,128,128]{1,2,0:T(8,128)S(1)} custom-call(f32[2,128,128]{2,1,0:T(8,128)S(1)} %get-tuple-element.26), custom_call_target="InvertDiagBlocksLowerTriangular" | custom-call | tf_op jit(solution)/shard_map/jit(_cho_solve)/triangular_solve | solution.py:28
  367.8 4.4 convolution_subtract_fusion
  373.5 4.3 fusion.134
  377.8 45.7 %all-reduce.7.cloned.1.call-done = f32[256,256]{0,1:T(8,128)} async-done(((f32[256,256]{0,1:T(8,128)}), f32[256,256]{0,1:T(8,128)}) %all-reduce.7.cloned.1.call-update) | async-done | bytes 262160 | tf_op jit(solution)/shard_map/psum | solution.py:32
  424.1 8.2 %collective-permute-done.22 = f32[256,256]{0,1:T(8,128)S(1)} collective-permute-done((f32[256,256]{0,1:T(8,128)}, f32[256,256]{0,1:T(8,128)S(1)}, u32[]{:S(2)}, u32[]{:S(2)}) %collective-permute-start.22) | collective-permute-done | bytes 262176 | tf_op jit(solution)/shard_map/ppermute | solution.py:10
  433.9 7.2 %collective-permute-done.23 = f32[256,256]{0,1:T(8,128)S(1)} collective-permute-done((f32[256,256]{0,1:T(8,128)S(1)}, f32[256,256]{0,1:T(8,128)S(1)}, u32[]{:S(2)}, u32[]{:S(2)}) %collective-permute-start.23) | collective-permute-done | bytes 262176 | tf_op jit(solution)/shard_map/ppermute | solution.py:10
  443.4 6.3 %collective-permute-done.24 = f32[256,256]{0,1:T(8,128)S(1)} collective-permute-done((f32[256,256]{0,1:T(8,128)S(1)}, f32[256,256]{0,1:T(8,128)S(1)}, u32[]{:S(2)}, u32[]{:S(2)}) %collective-permute-start.24) | collective-permute-done | bytes 262176 | tf_op jit(solution)/shard_map/ppermute | solution.py:10
  451.3 4.8 collective-permute-done.25
  456.2 3.3 collective-permute-start.26
  459.9 8.0 %collective-permute-done.26 = f32[256,256]{0,1:T(8,128)S(1)} collective-permute-done((f32[256,256]{0,1:T(8,128)S(1)}, f32[256,256]{0,1:T(8,128)S(1)}, u32[]{:S(2)}, u32[]{:S(2)}) %collective-permute-start.26) | collective-permute-done | bytes 262176 | tf_op jit(solution)/shard_map/ppermute | solution.py:10
  467.9 5.8 %collective-permute-start.27 = (f32[256,256]{0,1:T(8,128)S(1)}, f32[256,256]{0,1:T(8,128)S(1)}, u32[]{:S(2)}, u32[]{:S(2)}) collective-permute-start(f32[256,256]{0,1:T(8,128)S(1)} %add.201), channel_id=1, source_target_pairs={{0,128},{4,132},{8,136},{12,140},{16,144},{20,148},{24,152},{28,15... | collective-permute-start | bytes 786440 | tf_op jit(solution)/shard_map/ppermute | solution.py:10
  473.7 3.1 pad_maximum_fusion
  476.8 7.7 %collective-permute-done.27 = f32[256,256]{0,1:T(8,128)S(1)} collective-permute-done((f32[256,256]{0,1:T(8,128)S(1)}, f32[256,256]{0,1:T(8,128)S(1)}, u32[]{:S(2)}, u32[]{:S(2)}) %collective-permute-start.27) | collective-permute-done | bytes 262176 | tf_op jit(solution)/shard_map/ppermute | solution.py:10
  484.7 11.7 %cholesky.240 = f32[128,128]{1,0:T(8,128)S(1)} custom-call(f32[128,128]{1,0:T(8,128)S(1)} %cholesky.276), custom_call_target="Cholesky" | custom-call | tf_op jit(solution)/shard_map/jit(cholesky)/cholesky | solution.py:81
  496.5 9.8 %custom-call.22 = f32[1,128,128]{1,2,0:T(8,128)S(1)} custom-call(f32[1,128,128]{2,1,0:T(8,128)S(1)} %get-tuple-element.59), custom_call_target="InvertDiagBlocksLowerTriangular" | custom-call | tf_op jit(solution)/shard_map/jit(cholesky)/cholesky | solution.py:81
  506.8 11.7 %cholesky.257 = f32[128,128]{1,0:T(8,128)S(1)} custom-call(f32[128,128]{1,0:T(8,128)S(1)} %convolution_subtract_fusion.6), custom_call_target="Cholesky" | custom-call | tf_op jit(solution)/shard_map/jit(cholesky)/cholesky | solution.py:81
  (172 shorter events, 72.7 us)
Async XLA Ops:
  7.2 1.9 copy-start
  7.2 68.5 %all-reduce.11.cloned.1.call-start = ((), (), s32[]{:S(2)}) async-start(), calls=%async_computation.2 | async-start | bytes 1048576 | tf_op jit(solution)/shard_map/psum | solution.py:32
  9.1 2.5 copy-start.13
  11.6 7.1 %copy-start.8 = (f32[2048,256]{1,0:T(8,128)}, f32[2048,256]{1,0:T(8,128)S(1)}, u32[]{:S(2)}) copy-start(f32[2048,256]{1,0:T(8,128)S(1)} %fusion.24) | copy-start | bytes 6291460
  18.8 1.3 copy-start.11
  25.2 211.9 %all-reduce.9.cloned.1.call-start = ((), (), s32[]{:S(2)}) async-start(), calls=%async_computation.1 | async-start | bytes 1572864 | tf_op jit(solution)/shard_map/psum | solution.py:32
  75.7 9.4 %collective-permute-start = (f32[256,256]{0,1:T(8,128)}, f32[256,256]{0,1:T(8,128)S(1)}, u32[]{:S(2)}, u32[]{:S(2)}) collective-permute-start(f32[256,256]{0,1:T(8,128)} %get-tuple-element.46), channel_id=1, source_target_pairs={{0,4},{4,0},{8,12},{12,8},{16,20},{20,16},{24,28},{28,24},{32,36},... | collective-permute-start | bytes 786440 | tf_op jit(solution)/shard_map/ppermute | solution.py:10
  76.3 13.9 %collective-permute-start.4 = (f32[256,256]{1,0:T(8,128)}, f32[256,256]{1,0:T(8,128)S(1)}, u32[]{:S(2)}, u32[]{:S(2)}) collective-permute-start(f32[256,256]{1,0:T(8,128)} %get-tuple-element.47), channel_id=1, source_target_pairs={{0,4},{4,0},{8,12},{12,8},{16,20},{20,16},{24,28},{28,24},{32,36},... | collective-permute-start | bytes 786440 | tf_op jit(solution)/shard_map/ppermute | solution.py:10
  86.1 7.2 %collective-permute-start.1 = (f32[256,256]{0,1:T(8,128)S(1)}, f32[256,256]{0,1:T(8,128)S(1)}, u32[]{:S(2)}, u32[]{:S(2)}) collective-permute-start(f32[256,256]{0,1:T(8,128)S(1)} %add.170), channel_id=1, source_target_pairs={{0,8},{4,12},{8,0},{12,4},{16,24},{20,28},{24,16},{28,20},{32,40},... | collective-permute-start | bytes 786440 | tf_op jit(solution)/shard_map/ppermute | solution.py:10
  91.1 9.3 %collective-permute-start.5 = (f32[256,256]{1,0:T(8,128)S(1)}, f32[256,256]{1,0:T(8,128)S(1)}, u32[]{:S(2)}, u32[]{:S(2)}) collective-permute-start(f32[256,256]{1,0:T(8,128)S(1)} %add.175), channel_id=1, source_target_pairs={{0,8},{4,12},{8,0},{12,4},{16,24},{20,28},{24,16},{28,20},{32,40},... | collective-permute-start | bytes 786440 | tf_op jit(solution)/shard_map/ppermute | solution.py:10
  93.3 13.6 %collective-permute-start.2 = (f32[256,256]{0,1:T(8,128)S(1)}, f32[256,256]{0,1:T(8,128)S(1)}, u32[]{:S(2)}, u32[]{:S(2)}) collective-permute-start(f32[256,256]{0,1:T(8,128)S(1)} %add.171), channel_id=1, source_target_pairs={{0,16},{4,20},{8,24},{12,28},{16,0},{20,4},{24,8},{28,12},{32,48},... | collective-permute-start | bytes 786440 | tf_op jit(solution)/shard_map/ppermute | solution.py:10
  95.6 13.0 %copy-start.9 = (f32[2048,256]{1,0:T(8,128)S(1)}, f32[2048,256]{1,0:T(8,128)}, u32[]{:S(2)}) copy-start(f32[2048,256]{1,0:T(8,128)} %copy-done.8) | copy-start | bytes 6291460
  98.0 10.6 %copy-start.5 = (f32[2048,256]{1,0:T(8,128)}, f32[2048,256]{1,0:T(8,128)S(1)}, u32[]{:S(2)}) copy-start(f32[2048,256]{1,0:T(8,128)S(1)} %fusion) | copy-start | bytes 6291460
  100.4 12.8 %collective-permute-start.6 = (f32[256,256]{1,0:T(8,128)S(1)}, f32[256,256]{1,0:T(8,128)S(1)}, u32[]{:S(2)}, u32[]{:S(2)}) collective-permute-start(f32[256,256]{1,0:T(8,128)S(1)} %add.176), channel_id=1, source_target_pairs={{0,16},{4,20},{8,24},{12,28},{16,0},{20,4},{24,8},{28,12},{32,48},... | collective-permute-start | bytes 786440 | tf_op jit(solution)/shard_map/ppermute | solution.py:10
  106.9 7.0 %collective-permute-start.3 = (f32[256,256]{0,1:T(8,128)S(1)}, f32[256,256]{0,1:T(8,128)S(1)}, u32[]{:S(2)}, u32[]{:S(2)}) collective-permute-start(f32[256,256]{0,1:T(8,128)S(1)} %add.172), channel_id=1, source_target_pairs={{0,32},{4,36},{8,40},{12,44},{16,48},{20,52},{24,56},{28,60},{32,0... | collective-permute-start | bytes 786440 | tf_op jit(solution)/shard_map/ppermute | solution.py:10
  113.3 60.8 %collective-permute-start.7 = (f32[256,256]{1,0:T(8,128)S(1)}, f32[256,256]{1,0:T(8,128)S(1)}, u32[]{:S(2)}, u32[]{:S(2)}) collective-permute-start(f32[256,256]{1,0:T(8,128)S(1)} %add.177), channel_id=1, source_target_pairs={{0,32},{4,36},{8,40},{12,44},{16,48},{20,52},{24,56},{28,60},{32,0... | collective-permute-start | bytes 786440 | tf_op jit(solution)/shard_map/ppermute | solution.py:10
  176.1 4.3 copy-start.12
  180.5 4.3 copy-start.1
  180.5 4.3 copy-start.6
  189.1 234.4 %all-reduce.7.cloned.1.call-start = ((), (), s32[]{:S(2)}) async-start(), calls=%async_computation | async-start | bytes 524288 | tf_op jit(solution)/shard_map/psum | solution.py:32
  237.1 9.4 %collective-permute-start.12 = (f32[256,256]{0,1:T(8,128)}, f32[256,256]{0,1:T(8,128)S(1)}, u32[]{:S(2)}, u32[]{:S(2)}) collective-permute-start(f32[256,256]{0,1:T(8,128)} %get-tuple-element.45), channel_id=1, source_target_pairs={{0,4},{4,0},{8,12},{12,8},{16,20},{20,16},{24,28},{28,24},{32,36},... | collective-permute-start | bytes 786440 | tf_op jit(solution)/shard_map/ppermute | solution.py:10
  237.7 14.4 %collective-permute-start.8 = (f32[256,256]{1,0:T(8,128)}, f32[256,256]{1,0:T(8,128)S(1)}, u32[]{:S(2)}, u32[]{:S(2)}) collective-permute-start(f32[256,256]{1,0:T(8,128)} %get-tuple-element.43), channel_id=1, source_target_pairs={{0,4},{4,0},{8,12},{12,8},{16,20},{20,16},{24,28},{28,24},{32,36},... | collective-permute-start | bytes 786440 | tf_op jit(solution)/shard_map/ppermute | solution.py:10
  239.1 18.0 %collective-permute-start.17 = (f32[256,256]{1,0:T(8,128)}, f32[256,256]{1,0:T(8,128)S(1)}, u32[]{:S(2)}, u32[]{:S(2)}) collective-permute-start(f32[256,256]{1,0:T(8,128)} %get-tuple-element.44), channel_id=1, source_target_pairs={{0,4},{4,0},{8,12},{12,8},{16,20},{20,16},{24,28},{28,24},{32,36},... | collective-permute-start | bytes 786440 | tf_op jit(solution)/shard_map/ppermute | solution.py:10
  247.5 11.3 %collective-permute-start.13 = (f32[256,256]{0,1:T(8,128)S(1)}, f32[256,256]{0,1:T(8,128)S(1)}, u32[]{:S(2)}, u32[]{:S(2)}) collective-permute-start(f32[256,256]{0,1:T(8,128)S(1)} %add.186), channel_id=1, source_target_pairs={{0,8},{4,12},{8,0},{12,4},{16,24},{20,28},{24,16},{28,20},{32,40},... | collective-permute-start | bytes 786440 | tf_op jit(solution)/shard_map/ppermute | solution.py:10
  253.1 8.2 %collective-permute-start.9 = (f32[256,256]{1,0:T(8,128)S(1)}, f32[256,256]{1,0:T(8,128)S(1)}, u32[]{:S(2)}, u32[]{:S(2)}) collective-permute-start(f32[256,256]{1,0:T(8,128)S(1)} %add.182), channel_id=1, source_target_pairs={{0,8},{4,12},{8,0},{12,4},{16,24},{20,28},{24,16},{28,20},{32,40},... | collective-permute-start | bytes 786440 | tf_op jit(solution)/shard_map/ppermute | solution.py:10
  258.1 9.3 %collective-permute-start.18 = (f32[256,256]{1,0:T(8,128)S(1)}, f32[256,256]{1,0:T(8,128)S(1)}, u32[]{:S(2)}, u32[]{:S(2)}) collective-permute-start(f32[256,256]{1,0:T(8,128)S(1)} %add.192), channel_id=1, source_target_pairs={{0,8},{4,12},{8,0},{12,4},{16,24},{20,28},{24,16},{28,20},{32,40},... | collective-permute-start | bytes 786440 | tf_op jit(solution)/shard_map/ppermute | solution.py:10
  258.8 15.1 %collective-permute-start.14 = (f32[256,256]{0,1:T(8,128)S(1)}, f32[256,256]{0,1:T(8,128)S(1)}, u32[]{:S(2)}, u32[]{:S(2)}) collective-permute-start(f32[256,256]{0,1:T(8,128)S(1)} %add.187), channel_id=1, source_target_pairs={{0,16},{4,20},{8,24},{12,28},{16,0},{20,4},{24,8},{28,12},{32,48},... | collective-permute-start | bytes 786440 | tf_op jit(solution)/shard_map/ppermute | solution.py:10
  261.3 18.2 %collective-permute-start.10 = (f32[256,256]{1,0:T(8,128)S(1)}, f32[256,256]{1,0:T(8,128)S(1)}, u32[]{:S(2)}, u32[]{:S(2)}) collective-permute-start(f32[256,256]{1,0:T(8,128)S(1)} %add.183), channel_id=1, source_target_pairs={{0,16},{4,20},{8,24},{12,28},{16,0},{20,4},{24,8},{28,12},{32,48},... | collective-permute-start | bytes 786440 | tf_op jit(solution)/shard_map/ppermute | solution.py:10
  267.4 16.7 %collective-permute-start.19 = (f32[256,256]{1,0:T(8,128)S(1)}, f32[256,256]{1,0:T(8,128)S(1)}, u32[]{:S(2)}, u32[]{:S(2)}) collective-permute-start(f32[256,256]{1,0:T(8,128)S(1)} %add.193), channel_id=1, source_target_pairs={{0,16},{4,20},{8,24},{12,28},{16,0},{20,4},{24,8},{28,12},{32,48},... | collective-permute-start | bytes 786440 | tf_op jit(solution)/shard_map/ppermute | solution.py:10
  274.0 11.8 %collective-permute-start.15 = (f32[256,256]{0,1:T(8,128)S(1)}, f32[256,256]{0,1:T(8,128)S(1)}, u32[]{:S(2)}, u32[]{:S(2)}) collective-permute-start(f32[256,256]{0,1:T(8,128)S(1)} %add.188), channel_id=1, source_target_pairs={{0,32},{4,36},{8,40},{12,44},{16,48},{20,52},{24,56},{28,60},{32,0... | collective-permute-start | bytes 786440 | tf_op jit(solution)/shard_map/ppermute | solution.py:10
  279.6 8.9 %collective-permute-start.11 = (f32[256,256]{1,0:T(8,128)S(1)}, f32[256,256]{1,0:T(8,128)S(1)}, u32[]{:S(2)}, u32[]{:S(2)}) collective-permute-start(f32[256,256]{1,0:T(8,128)S(1)} %add.184), channel_id=1, source_target_pairs={{0,32},{4,36},{8,40},{12,44},{16,48},{20,52},{24,56},{28,60},{32,0... | collective-permute-start | bytes 786440 | tf_op jit(solution)/shard_map/ppermute | solution.py:10
  284.1 13.0 %collective-permute-start.20 = (f32[256,256]{1,0:T(8,128)S(1)}, f32[256,256]{1,0:T(8,128)S(1)}, u32[]{:S(2)}, u32[]{:S(2)}) collective-permute-start(f32[256,256]{1,0:T(8,128)S(1)} %add.194), channel_id=1, source_target_pairs={{0,32},{4,36},{8,40},{12,44},{16,48},{20,52},{24,56},{28,60},{32,0... | collective-permute-start | bytes 786440 | tf_op jit(solution)/shard_map/ppermute | solution.py:10
  285.8 18.0 %collective-permute-start.16 = (f32[256,256]{0,1:T(8,128)S(1)}, f32[256,256]{0,1:T(8,128)}, u32[]{:S(2)}, u32[]{:S(2)}) collective-permute-start(f32[256,256]{0,1:T(8,128)S(1)} %add.189), channel_id=1, source_target_pairs={{0,64},{4,68},{8,72},{12,76},{16,80},{20,84},{24,88},{28,92},{32,9... | collective-permute-start | bytes 786440 | tf_op jit(solution)/shard_map/ppermute | solution.py:10
  297.2 68.5 %collective-permute-start.21 = (f32[256,256]{1,0:T(8,128)S(1)}, f32[256,256]{1,0:T(8,128)S(1)}, u32[]{:S(2)}, u32[]{:S(2)}) collective-permute-start(f32[256,256]{1,0:T(8,128)S(1)} %add.195), channel_id=1, source_target_pairs={{0,64},{4,68},{8,72},{12,76},{16,80},{20,84},{24,88},{28,92},{32,9... | collective-permute-start | bytes 786440 | tf_op jit(solution)/shard_map/ppermute | solution.py:10
  367.8 5.8 %copy-start.7 = (f32[2048,256]{1,0:T(8,128)S(1)}, f32[2048,256]{1,0:T(8,128)}, u32[]{:S(2)}) copy-start(f32[2048,256]{1,0:T(8,128)} %copy-done.5) | copy-start | bytes 6291460
  372.2 1.4 copy-start.3
  423.5 36.0 %copy-start.10 = (f32[2048,256]{1,0:T(8,128)S(1)}, f32[2048,256]{1,0:T(8,128)}, u32[]{:S(2)}) copy-start(f32[2048,256]{1,0:T(8,128)} %copy-done.8) | copy-start | bytes 6291460
  423.5 8.8 %collective-permute-start.22 = (f32[256,256]{0,1:T(8,128)}, f32[256,256]{0,1:T(8,128)S(1)}, u32[]{:S(2)}, u32[]{:S(2)}) collective-permute-start(f32[256,256]{0,1:T(8,128)} %all-reduce.7.cloned.1.call-done), channel_id=1, source_target_pairs={{0,4},{4,0},{8,12},{12,8},{16,20},{20,16},{24,28},{28,24},{32,36},... | collective-permute-start | bytes 786440 | tf_op jit(solution)/shard_map/ppermute | solution.py:10
  433.3 7.8 %collective-permute-start.23 = (f32[256,256]{0,1:T(8,128)S(1)}, f32[256,256]{0,1:T(8,128)S(1)}, u32[]{:S(2)}, u32[]{:S(2)}) collective-permute-start(f32[256,256]{0,1:T(8,128)S(1)} %add.197), channel_id=1, source_target_pairs={{0,8},{4,12},{8,0},{12,4},{16,24},{20,28},{24,16},{28,20},{32,40},... | collective-permute-start | bytes 786440 | tf_op jit(solution)/shard_map/ppermute | solution.py:10
  441.2 8.5 %collective-permute-start.24 = (f32[256,256]{0,1:T(8,128)S(1)}, f32[256,256]{0,1:T(8,128)S(1)}, u32[]{:S(2)}, u32[]{:S(2)}) collective-permute-start(f32[256,256]{0,1:T(8,128)S(1)} %add.198), channel_id=1, source_target_pairs={{0,16},{4,20},{8,24},{12,28},{16,0},{20,4},{24,8},{28,12},{32,48},... | collective-permute-start | bytes 786440 | tf_op jit(solution)/shard_map/ppermute | solution.py:10
  449.7 6.5 %collective-permute-start.25 = (f32[256,256]{0,1:T(8,128)S(1)}, f32[256,256]{0,1:T(8,128)S(1)}, u32[]{:S(2)}, u32[]{:S(2)}) collective-permute-start(f32[256,256]{0,1:T(8,128)S(1)} %add.199), channel_id=1, source_target_pairs={{0,32},{4,36},{8,40},{12,44},{16,48},{20,52},{24,56},{28,60},{32,0... | collective-permute-start | bytes 786440 | tf_op jit(solution)/shard_map/ppermute | solution.py:10
  456.2 17.5 %copy-start.2 = (f32[2048,256]{1,0:T(8,128)S(1)}, f32[2048,256]{1,0:T(8,128)}, u32[]{:S(2)}) copy-start(f32[2048,256]{1,0:T(8,128)} %copy-done.1) | copy-start | bytes 6291460
  456.2 17.5 %copy-start.4 = (f32[2048,256]{1,0:T(8,128)S(1)}, f32[2048,256]{1,0:T(8,128)}, u32[]{:S(2)}) copy-start(f32[2048,256]{1,0:T(8,128)} %copy-done.3) | copy-start | bytes 6291460
  456.2 11.7 %collective-permute-start.26 = (f32[256,256]{0,1:T(8,128)S(1)}, f32[256,256]{0,1:T(8,128)S(1)}, u32[]{:S(2)}, u32[]{:S(2)}) collective-permute-start(f32[256,256]{0,1:T(8,128)S(1)} %add.200), channel_id=1, source_target_pairs={{0,64},{4,68},{8,72},{12,76},{16,80},{20,84},{24,88},{28,92},{32,9... | collective-permute-start | bytes 786440 | tf_op jit(solution)/shard_map/ppermute | solution.py:10
  467.9 16.6 %collective-permute-start.27 = (f32[256,256]{0,1:T(8,128)S(1)}, f32[256,256]{0,1:T(8,128)S(1)}, u32[]{:S(2)}, u32[]{:S(2)}) collective-permute-start(f32[256,256]{0,1:T(8,128)S(1)} %add.201), channel_id=1, source_target_pairs={{0,128},{4,132},{8,136},{12,140},{16,144},{20,148},{24,152},{28,15... | collective-permute-start | bytes 786440 | tf_op jit(solution)/shard_map/ppermute | solution.py:10
Sparse Core Ops, SparseCore 0:
  25.3 50.3 all-reduce.10
  189.2 47.8 all-reduce.8
  378.0 45.4 all-reduce.6
where the time goes:
time: 538 us; the launch traced here: 529 us
  waiting for transfers between devices  241 us (45%)
  other arithmetic  155 us (29%)
  matrix products  55.8 us (10%)
  starting transfers between devices  44.3 us (8%)
  between operations  18.6 us (3%)
  local copies, waits for them, and re-layouts  14 us (3%)
    psum x3, waiting for transfers between devices, group_total(): summed = lax.psum(partial_value, 'rows')  144 us
    another operation x20, other arithmetic, on_device(): jnp.linalg.cholesky(identity + gram_matrix / node_rows[level_index])  104 us
    ppermute x28, waiting for transfers between devices, partner(): lax.ppermute(value, axis, [(i, i ^ 1 << bit) for i in range(lax.axis_size...  96.5 us
    ppermute x28, starting transfers between devices, partner(): lax.ppermute(value, axis, [(i, i ^ 1 << bit) for i in range(lax.axis_size...  44.2 us
    another operation x3, other arithmetic, solve_with(): return jax.scipy.linalg.cho_solve((factor, True), right_side)  39.6 us
    dot_general x6, matrix products, project(): jnp.einsum('nr,ns->rs', left, right, precision=highest, preferred_element...  27.2 us
    dot_general x3, matrix products, on_device(): jnp.dot(bases[prior_index], coefficients[prior_index, level_index], preci...  14.2 us
  transfers between devices with their start and end apart: 31, of which 22 were waited for; matrix products, arithmetic and copies ran while one was open for 27% of the time, Pallas kernels for 0%

commit v1 on v0

v1 whole, which is shorter than its diff:
```python
import functools

import jax
import jax.numpy as jnp
from jax import lax
from jax.experimental import pallas as pl
from jax.experimental.pallas import tpu as pltpu
from jax.sharding import PartitionSpec as P

f32 = jnp.float32
bf16 = jnp.bfloat16
highest = lax.Precision.HIGHEST
MESH = pl.DeviceIdType.MESH
RANK = 256
HALF = 128
CHIPS = 32
SLAB = 8
NODE_BRANCHES = 16
CHUNK = 256


def mm(left, right, contract=(1, 0)):
    return lax.dot_general(
        left, right, (((contract[0],), (contract[1],)), ((), ())),
        precision=highest, preferred_element_type=f32,
    )


def place():
    branch = lax.axis_index("branch")
    row = lax.axis_index("rows")
    chip = lax.rem(branch, NODE_BRANCHES) * 2 + row // 2
    return branch, row, chip, lax.rem(row, 2)


def chip_id(branch, chip, core):
    base = branch - lax.rem(branch, NODE_BRANCHES)
    return (base + chip // 2, lax.rem(chip, 2) * 2 + core)


def rows_kernel(scale, ids, points, noise, landmarks, m1, m2, m3, scaled, products):
    step = pl.program_id(0)
    columns = jnp.concatenate(
        [points[...], noise[...], jnp.zeros((4, CHUNK), f32)], axis=0
    ).T
    weight = 1.0 / columns[:, 3:4]
    units, weighted = [], []
    for level, mixing in enumerate((m1, m2, m3)):
        spread = None
        for c in range(3):
            mark = landmarks[pl.ds(ids[level], 1), c, :]
            offset = columns[:, c:c + 1] - mark
            spread = offset * offset if spread is None else spread + offset * offset
        kernel = jnp.exp(-spread * scale)
        unit = mm(kernel, mixing[0])
        units.append(unit)
        weighted.append(unit * weight)
        scaled[level] = weighted[level]

    @pl.when(step == 0)
    def _():
        products[...] = jnp.zeros_like(products)

    for index, (i, j) in enumerate(PAIRS):
        product = mm(weighted[i], units[j], (0, 0))
        products[0, index] += product[:, :HALF]
        products[1, index] += product[:, HALF:]


PAIRS = ((0, 0), (0, 1), (0, 2), (1, 1), (1, 2), (2, 2))


def local_rows(ids, points, noise, landmarks, mixing):
    rows = points.shape[1]
    length_scale = 0.6 * RANK ** (-1.0 / 3.0)
    scale = 1.0 / (2.0 * length_scale * length_scale)
    mix = [
        pl.BlockSpec((1, RANK, RANK), functools.partial(lambda n, i, ids: (ids[n], 0, 0), n))
        for n in range(3)
    ]
    return pl.pallas_call(
        functools.partial(rows_kernel, scale),
        grid_spec=pltpu.PrefetchScalarGridSpec(
            num_scalar_prefetch=1,
            grid=(rows // CHUNK,),
            in_specs=[
                pl.BlockSpec((3, CHUNK), lambda i, ids: (0, i)),
                pl.BlockSpec((1, CHUNK), lambda i, ids: (0, i)),
                pl.BlockSpec((7, 3, RANK), lambda i, ids: (0, 0, 0)),
            ] + mix,
            out_specs=[
                pl.BlockSpec((3, CHUNK, RANK), lambda i, ids: (0, i, 0)),
                pl.BlockSpec((2, 6, RANK, HALF), lambda i, ids: (0, 0, 0, 0)),
            ],
        ),
        out_shape=[
            jax.ShapeDtypeStruct((3, rows, RANK), f32),
            jax.ShapeDtypeStruct((2, 6, RANK, HALF), f32),
        ],
        name="local_rows",
    )(ids, points, noise[None], landmarks, mixing, mixing, mixing)


def greet(peers):
    barrier = pltpu.get_barrier_semaphore()
    for peer in peers:
        pl.semaphore_signal(barrier, inc=1, device_id=peer, device_id_type=MESH)
    return len(peers)


def greet_chips(branch, chip, core):
    barrier = pltpu.get_barrier_semaphore()

    def one(k, carry):
        pl.semaphore_signal(
            barrier, inc=1, device_id=chip_id(branch, chip ^ k, core), device_id_type=MESH
        )
        return carry

    lax.fori_loop(1, CHIPS, one, 0)


def send(src, dst, send_sem, recv_sem, peer):
    copy = pltpu.make_async_remote_copy(
        src_ref=src, dst_ref=dst, send_sem=send_sem, recv_sem=recv_sem,
        device_id=peer, device_id_type=MESH,
    )
    copy.start()
    return copy


def gather_slabs(full, mine, branch, chip, core, other, sems, first):
    rows = pl.ds(pl.multiple_of(chip * SLAB, SLAB), SLAB)
    full[core, :, rows, :] = mine[...]

    def one(k, carry):
        send(mine, full.at[core, :, rows, :], sems.at[first], sems.at[first + 1],
             chip_id(branch, chip ^ k, core))
        return carry

    lax.fori_loop(1, CHIPS, one, 0)
    rest = full.at[core, :, pl.ds(0, RANK - SLAB), :]
    pltpu.make_async_copy(rest, rest, sems.at[first + 1]).wait()
    pltpu.make_async_copy(rest, rest, sems.at[first]).wait()
    send(full.at[core], full.at[core], sems.at[first + 2], sems.at[first + 3], other).wait()


def reduce_kernel(products, full, slab, paired, total, landed, mine, sems):
    branch, row, chip, core = place()
    other = (branch, row + 1 - 2 * core)
    n = greet([other])
    greet_chips(branch, chip, core)
    pl.semaphore_wait(pltpu.get_barrier_semaphore(), n + CHIPS - 1)
    send(products.at[1 - core], paired, sems.at[0], sems.at[1], other).wait()
    total[...] = products[core] + paired[...]

    def one(k, carry):
        peer = chip ^ k
        rows = pl.ds(pl.multiple_of(peer * SLAB, SLAB), SLAB)
        send(total.at[:, rows, :], landed.at[k], sems.at[2], sems.at[3],
             chip_id(branch, peer, core))
        return carry

    lax.fori_loop(1, CHIPS, one, 0)
    rest = landed.at[pl.ds(1, CHIPS - 1)]
    pltpu.make_async_copy(rest, rest, sems.at[3]).wait()
    pltpu.make_async_copy(rest, rest, sems.at[2]).wait()
    value = total[:, pl.ds(pl.multiple_of(chip * SLAB, SLAB), SLAB), :]
    for k in range(1, CHIPS):
        value = value + landed[k]
    mine[...] = value[:3]
    slab[...] = value[3:]
    gather_slabs(full, mine, branch, chip, core, other, sems, 4)


def reduce_products(products):
    return pl.pallas_call(
        reduce_kernel,
        out_shape=[
            jax.ShapeDtypeStruct((2, 3, RANK, HALF), f32),
            jax.ShapeDtypeStruct((3, SLAB, HALF), f32),
        ],
        in_specs=[pl.BlockSpec(memory_space=pltpu.VMEM)],
        out_specs=[pl.BlockSpec(memory_space=pltpu.VMEM)] * 2,
        scratch_shapes=[
            pltpu.VMEM((6, RANK, HALF), f32),
            pltpu.VMEM((6, RANK, HALF), f32),
            pltpu.VMEM((CHIPS, 6, SLAB, HALF), f32),
            pltpu.VMEM((3, SLAB, HALF), f32),
            pltpu.SemaphoreType.DMA((8,)),
        ],
        compiler_params=pltpu.CompilerParams(collective_id=0, has_side_effects=True),
        name="reduce_products",
    )(products)


def join_kernel(bit, gathered, slabs, *refs):
    if gathered < slabs.shape[0]:
        full, slab, landed, mine, sems = refs
    else:
        full, landed, mine, sems = refs
    branch, row, chip, core = place()
    other = (branch, row + 1 - 2 * core)
    match = (branch ^ bit, row)
    n = greet([other, match])
    greet_chips(branch, chip, core)
    pl.semaphore_wait(pltpu.get_barrier_semaphore(), n + CHIPS - 1)
    send(slabs, landed, sems.at[0], sems.at[1], match).wait()
    value = slabs[...] + landed[...]
    mine[...] = value[:gathered]
    if gathered < slabs.shape[0]:
        slab[...] = value[gathered:]
    gather_slabs(full, mine, branch, chip, core, other, sems, 2)


def join_halves(slabs, bit, gathered, number):
    count = slabs.shape[0]
    out = [jax.ShapeDtypeStruct((2, gathered, RANK, HALF), f32)]
    if gathered < count:
        out.append(jax.ShapeDtypeStruct((count - gathered, SLAB, HALF), f32))
    return pl.pallas_call(
        functools.partial(join_kernel, bit, gathered),
        out_shape=out,
        in_specs=[pl.BlockSpec(memory_space=pltpu.VMEM)],
        out_specs=[pl.BlockSpec(memory_space=pltpu.VMEM)] * len(out),
        scratch_shapes=[
            pltpu.VMEM((count, SLAB, HALF), f32),
            pltpu.VMEM((gathered, SLAB, HALF), f32),
            pltpu.SemaphoreType.DMA((6,)),
        ],
        compiler_params=pltpu.CompilerParams(collective_id=number, has_side_effects=True),
        name="join_halves",
    )(slabs)


def split3(x):
    a = x.astype(bf16); r = x - a.astype(f32)
    b = r.astype(bf16); c = (r - b.astype(f32)).astype(bf16)
    return a, b, c

def factor(T, W):
    def super_panel(s, carry):
        r0 = pl.multiple_of(s * 32, 32)
        tile = pl.multiple_of((s // 4) * 128, 128)
        block = T[pl.ds(r0, 32), pl.ds(tile, 128)]
        W[:, 0:128] = pltpu.roll(block, lax.rem(128 - lax.rem(s, 4) * 32, 128), 1)
        W[:, 128:640] = T[pl.ds(r0, 32), :]
        for p in range(4):
            k0 = 8 * p
            cols = [jnp.broadcast_to(W[k0:32, k0 + m:k0 + m + 1], (32 - k0, 128)) for m in range(8)]
            e = {}
            for m in range(8):
                for i in range(m, 8):
                    e[i, m] = jnp.broadcast_to(cols[m][i:i + 1, :], (8, 128))
            r, l = {}, {}
            for j in range(8):
                r[j] = lax.rsqrt(e[j, j])
                for i in range(j + 1, 8):
                    l[i, j] = e[i, j] * r[j]
                for k in range(j + 1, 8):
                    for i in range(k, 8):
                        e[i, k] = e[i, k] - l[i, j] * l[k, j]
            rows = []
            for i in range(8):
                tiles = []
                for c in range(5):
                    w = jnp.broadcast_to(W[k0 + i:k0 + i + 1, c * 128:(c + 1) * 128], (8, 128))
                    for k in range(i):
                        w = w - l[i, k] * rows[k][c]
                    tiles.append(w * r[i])
                rows.append(tiles)
            below = []
            for t in range(1, 4 - p):
                lc = []
                for j in range(8):
                    v = cols[j][8 * t:8 * t + 8, :]
                    for k in range(j):
                        v = v - l[j, k] * lc[k]
                    lc.append(v * r[j])
                for c in range(5):
                    w = W[k0 + 8 * t:k0 + 8 * t + 8, c * 128:(c + 1) * 128]
                    for j in range(8):
                        w = w - lc[j] * rows[j][c]
                    W[k0 + 8 * t:k0 + 8 * t + 8, c * 128:(c + 1) * 128] = w
            for i in range(8):
                for c in range(5):
                    W[k0 + i:k0 + i + 1, c * 128:(c + 1) * 128] = rows[i][c][0:1, :]
        done = W[:, 128:640]
        T[pl.ds(r0, 32), :] = done
        a, b, c = split3(done)
        left = jnp.concatenate([a, a, b, b, a, c], axis=0)
        right = jnp.concatenate([a, b, a, b, c, a], axis=0)
        def update(half):
            lo = half * 128
            prod = lax.dot_general(left[:, lo:lo + 128], right, (((0,), (0,)), ((), ())),
                                   preferred_element_type=f32)
            row = lax.broadcasted_iota(jnp.int32, (128, 512), 0) + lo
            T[lo:lo + 128, :] = T[lo:lo + 128, :] - jnp.where(row >= r0 + 32, prod, 0.0)
        @pl.when(s < 3)
        def _():
            update(0)
        @pl.when(s < 7)
        def _():
            update(1)
        return carry
    lax.fori_loop(0, 8, super_panel, 0)

def factor_capacitance(gram, rows, lower, T, W):
    i0 = lax.broadcasted_iota(jnp.int32, (RANK, RANK), 0)
    i1 = lax.broadcasted_iota(jnp.int32, (RANK, RANK), 1)
    identity = jnp.where(i0 == i1, 1.0, 0.0)
    T[:, 0:RANK] = identity + gram / rows
    T[:, RANK:2 * RANK] = identity
    factor(T, W)
    lower[...] = jnp.where(i0 >= i1, T[:, 0:RANK].T, 0.0)
    return T[:, RANK:2 * RANK]


def whole(full, index):
    return jnp.concatenate([full[0, index], full[1, index]], axis=1)


def minus(slab, left, right, rows, spare, chip, core):
    product = mm(left, right, (0, 0)) / rows
    spare[0] = product[:, :HALF]
    spare[1] = product[:, HALF:]
    return slab - spare[core, pl.ds(pl.multiple_of(chip * SLAB, SLAB), SLAB), :]


def finest_kernel(rows, full, slab, lower, c12, c13, left, T, W, spare):
    branch, row, chip, core = place()
    inverse = factor_capacitance(whole(full, 0), rows, lower, T, W)
    y12 = mm(inverse, whole(full, 1))
    y13 = mm(inverse, whole(full, 2))
    left[0] = minus(slab[0], y12, y12, rows, spare, chip, core)
    left[1] = minus(slab[1], y12, y13, rows, spare, chip, core)
    left[2] = minus(slab[2], y13, y13, rows, spare, chip, core)
    c12[...] = mm(inverse, y12, (0, 0)) / rows
    c13[...] = mm(inverse, y13, (0, 0)) / rows


def middle_kernel(rows, full, slab, lower, c23, left, T, W, spare):
    branch, row, chip, core = place()
    inverse = factor_capacitance(whole(full, 0), rows, lower, T, W)
    y23 = mm(inverse, whole(full, 1))
    left[0] = minus(slab[0], y23, y23, rows, spare, chip, core)
    c23[...] = mm(inverse, y23, (0, 0)) / rows


def coarsest_kernel(rows, full, lower, T, W):
    factor_capacitance(whole(full, 0), rows, lower, T, W)


def small(kernel, rows, args, outs, spare):
    scratch = [pltpu.VMEM((RANK, 2 * RANK), f32), pltpu.VMEM((32, 640), f32)]
    if spare:
        scratch.append(pltpu.VMEM((2, RANK, HALF), f32))
    return pl.pallas_call(
        functools.partial(kernel, rows),
        out_shape=[jax.ShapeDtypeStruct(o, f32) for o in outs],
        in_specs=[pl.BlockSpec(memory_space=pltpu.VMEM)] * len(args),
        out_specs=[pl.BlockSpec(memory_space=pltpu.VMEM)] * len(outs),
        scratch_shapes=scratch,
        name=kernel.__name__,
    )(*args)


def bases_kernel(scaled, c12, c13, c23, bases):
    first = scaled[0]
    second = scaled[1] - mm(first, c12[...])
    third = scaled[2] - mm(first, c13[...]) - mm(second, c23[...])
    bases[0] = first
    bases[1] = second
    bases[2] = third


def solve_bases(scaled, c12, c13, c23):
    rows = scaled.shape[1]
    square = pl.BlockSpec((RANK, RANK), lambda i: (0, 0))
    block = pl.BlockSpec((3, CHUNK, RANK), lambda i: (0, i, 0))
    return pl.pallas_call(
        bases_kernel,
        grid=(rows // CHUNK,),
        in_specs=[block, square, square, square],
        out_specs=block,
        out_shape=jax.ShapeDtypeStruct(scaled.shape, f32),
        name="solve_bases",
    )(scaled, c12, c13, c23)


def on_device(points, noise, landmarks, mixing):
    branch = lax.axis_index("branch")
    node_rows = float(NODE_BRANCHES * lax.axis_size("rows") * points.shape[1])
    ids = jnp.stack([3 + branch // 16, 1 + branch // 32, 0 * branch]).astype(jnp.int32)
    scaled, products = local_rows(ids, points, noise, landmarks, mixing)
    full, slab = reduce_products(products)
    square = (RANK, RANK)
    l1, c12, c13, left = small(
        finest_kernel, node_rows, (full, slab), (square, square, square, (3, SLAB, HALF)), True
    )
    full, slab = join_halves(left, 16, 2, 1)
    l2, c23, left = small(
        middle_kernel, 2 * node_rows, (full, slab), (square, square, (1, SLAB, HALF)), True
    )
    (full,) = join_halves(left, 32, 1, 2)
    (l3,) = small(coarsest_kernel, 4 * node_rows, (full,), (square,), False)
    bases = solve_bases(scaled, c12, c13, c23)
    return bases, jnp.stack([l1, l2, l3], axis=0)[None]


def solution(mesh):
    in_specs = (P(None, ("branch", "rows")), P(("branch", "rows")), P(), P())
    out_specs = (P(None, ("branch", "rows"), None), P("branch", None, None, None))
    return jax.shard_map(
        on_device, mesh=mesh, in_specs=in_specs, out_specs=out_specs, check_vma=False
    )
```

time: 538 us -> 152 us (0.28)
  the two profiles are of different devices: /device:TPU:8 before, /device:TPU:1 now
where the time goes in v1:
time: 152 us; the launch traced here: 151 us
  Pallas kernels  147 us (97%)
  other arithmetic  2.49 us (2%)
    pallas_call x3, Pallas kernels, small(): pl.pallas_call(functools.partial(kernel, rows), out_shape=[jax.ShapeDtype...  37.8 us
    pallas_call x1, Pallas kernels, reduce_products(): pl.pallas_call(reduce_kernel, out_shape=[jax.ShapeDtypeStruct((2, 3, RANK...  36.6 us
    pallas_call x2, Pallas kernels, join_halves(): pl.pallas_call(functools.partial(join_kernel, bit, gathered), out_shape=o...  35.8 us
    pallas_call x1, Pallas kernels, local_rows(): pl.pallas_call(functools.partial(rows_kernel, scale), grid_spec=pltpu.Pre...  25.5 us
    pallas_call x1, Pallas kernels, solve_bases(): pl.pallas_call(bases_kernel, grid=(rows // CHUNK,), in_specs=[block, squa...  11.1 us

profile of v1, /device:TPU:1, one launch (start us, length us, event | category | flops | bytes accessed | tf_op | source)
XLA Modules:
  0.0 151.3 jit_solution(4196503974659523350)
XLA Ops:
  0.7 0.6 pad_add_fusion.ids
  1.3 1.4 copy.6.landmarks
  2.6 25.5 %local_rows.1 = (f32[3,2048,256]{2,1,0:T(8,128)}, f32[2,6,256,128]{3,2,1,0:T(8,128)}) custom-call(s32[3]{0:T(128)} %pad_add_fusion.ids, f32[3,2048]{1,0:T(4,128)} %points.1, f32[1,2048]{1,0:T(1,128)} %bitcast.11, f32[7,3,256]{2,1,0:T(4,128)} %copy.6.landmarks, f32[7,256,256]{2,1,0:T(8,128)} %m3.1, f32[7,256,256]{2,1,0:T(8,128)} %m3.1, f32[7,256,256]{2,1,0:T(8,128)} %m3.1), custom_call_target="tpu_custom_call" | custom-call | tf_op jit(solution)/shard_map/local_rows/pallas_call | solution.py:81
  28.1 36.6 %reduce_products.1 = (f32[2,3,256,128]{3,2,1,0:T(8,128)}, f32[3,8,128]{2,1,0:T(8,128)}) custom-call(f32[2,6,256,128]{3,2,1,0:T(8,128)} %get-tuple-element.16.products), custom_call_target="tpu_custom_call" | custom-call | tf_op jit(solution)/shard_map/reduce_products/pallas_call | solution.py:177
  64.7 13.6 %finest_kernel.1 = (f32[256,256]{1,0:T(8,128)}, f32[256,256]{1,0:T(8,128)}, f32[256,256]{1,0:T(8,128)}, f32[3,8,128]{2,1,0:T(8,128)}) custom-call(f32[2,3,256,128]{3,2,1,0:T(8,128)} %get-tuple-element.17.full, f32[3,8,128]{2,1,0:T(8,128)} %get-tuple-element.18.slab), custom_call_target="tpu_custom_call" | custom-call | tf_op jit(solution)/shard_map/finest_kernel/pallas_call | solution.py:358
  78.3 18.3 %join_halves.2 = (f32[2,2,256,128]{3,2,1,0:T(8,128)}, f32[1,8,128]{2,1,0:T(8,128)}) custom-call(f32[3,8,128]{2,1,0:T(8,128)} %get-tuple-element.21.slabs), custom_call_target="tpu_custom_call" | custom-call | tf_op jit(solution)/shard_map/join_halves/pallas_call | solution.py:221
  96.5 12.6 %middle_kernel.1 = (f32[256,256]{1,0:T(8,128)}, f32[256,256]{1,0:T(8,128)}, f32[1,8,128]{2,1,0:T(8,128)}) custom-call(f32[2,2,256,128]{3,2,1,0:T(8,128)} %get-tuple-element.22.full, f32[1,8,128]{2,1,0:T(8,128)} %get-tuple-element.23.slab), custom_call_target="tpu_custom_call" | custom-call | tf_op jit(solution)/shard_map/middle_kernel/pallas_call | solution.py:358
  109.1 0.0 copy-start
  109.1 0.0 copy-start.1
  109.1 11.1 %solve_bases.1 = f32[3,2048,256]{2,1,0:T(8,128)} custom-call(f32[3,2048,256]{2,1,0:T(8,128)} %get-tuple-element.15.scaled, f32[256,256]{1,0:T(8,128)} %get-tuple-element.19.c12, f32[256,256]{1,0:T(8,128)} %get-tuple-element.20.c13, f32[256,256]{1,0:T(8,128)} %get-tuple-element.24.c23), custom_call_target="tpu_custom_call" | custom-call | tf_op jit(solution)/shard_map/solve_bases/pallas_call | solution.py:381
  120.2 17.5 %join_halves.3.full = f32[2,1,256,128]{3,2,1,0:T(8,128)} custom-call(f32[1,8,128]{2,1,0:T(8,128)} %get-tuple-element.27.slabs), custom_call_target="tpu_custom_call" | custom-call | tf_op jit(solution)/shard_map/join_halves/pallas_call | solution.py:221
  137.8 11.6 %coarsest_kernel.1 = f32[256,256]{1,0:T(8,128)} custom-call(f32[2,1,256,128]{3,2,1,0:T(8,128)} %join_halves.3.full), custom_call_target="tpu_custom_call" | custom-call | tf_op jit(solution)/shard_map/coarsest_kernel/pallas_call | solution.py:358
  149.4 0.0 copy-done
  149.4 0.0 copy-done.1
  149.4 1.9 %maximum_bitcast_fusion = f32[1,3,256,256]{3,2,1,0:T(8,128)} fusion(f32[1,256,256]{2,1,0:T(8,128)} %bitcast.8, f32[1,256,256]{2,1,0:T(8,128)S(1)} %bitcast.10, f32[1,256,256]{2,1,0:T(8,128)S(1)} %bitcast.9), kind=kLoop, calls=%fused_computation | loop fusion | flops 393216 | bytes 1572864 | tf_op jit(solution)/shard_map/broadcast_in_dim | solution.py:408
Async XLA Ops:
  109.1 40.3 %copy-start = (f32[256,256]{1,0:T(8,128)S(1)}, f32[256,256]{1,0:T(8,128)}, u32[]{:S(2)}) copy-start(f32[256,256]{1,0:T(8,128)} %get-tuple-element.25) | copy-start | bytes 786436
  109.1 40.3 %copy-start.1 = (f32[256,256]{1,0:T(8,128)S(1)}, f32[256,256]{1,0:T(8,128)}, u32[]{:S(2)}) copy-start(f32[256,256]{1,0:T(8,128)} %get-tuple-element.26) | copy-start | bytes 786436

commit v2 on v0

v2 whole, which is shorter than its diff:
```python
import functools

import jax
import jax.numpy as jnp
from jax import lax
from jax.experimental import pallas as pl
from jax.experimental.pallas import tpu as pltpu
from jax.sharding import PartitionSpec as P

f32 = jnp.float32
bf16 = jnp.bfloat16
highest = lax.Precision.HIGHEST
MESH = pl.DeviceIdType.MESH
RANK = 256
HALF = 128
CHIPS = 32
SLAB = 8
NODE_BRANCHES = 16
CHUNK = 512
BLOCKS = ((0, 0), (0, 1), (1, 1), (0, 2), (1, 2), (2, 2))
BATCHES = ((0, 1), (1, 3), (3, 6))


def mm(left, right, contract=(1, 0)):
    return lax.dot_general(
        left, right, (((contract[0],), (contract[1],)), ((), ())),
        precision=highest, preferred_element_type=f32,
    )


def place():
    branch = lax.axis_index("branch")
    row = lax.axis_index("rows")
    chip = lax.rem(branch, NODE_BRANCHES) * 2 + row // 2
    return branch, row, chip, lax.rem(row, 2)


def chip_id(branch, chip, core):
    base = branch - lax.rem(branch, NODE_BRANCHES)
    return (base + chip // 2, lax.rem(chip, 2) * 2 + core)


def split2(x):
    high = x.astype(bf16)
    return high, (x - high.astype(f32)).astype(bf16)


def split3(x):
    a = x.astype(bf16)
    r = x - a.astype(f32)
    b = r.astype(bf16)
    return a, b, (r - b.astype(f32)).astype(bf16)


def left3(parts, axis):
    return jnp.concatenate([parts[0], parts[0], parts[1]], axis=axis)


def right3(parts):
    return jnp.concatenate([parts[0], parts[1], parts[0]], axis=0)


def dot(left, right, contract=(1, 0)):
    return lax.dot_general(
        left, right, (((contract[0],), (contract[1],)), ((), ())), preferred_element_type=f32
    )


def super_panel(s, second, wide, T, W):
    r0 = pl.multiple_of(s * 32, 32)
    shift = lax.rem(s, 4) * 32
    own = HALF if second else 0
    others = [] if second else [HALF]
    if wide:
        others = others + ([2 * HALF, 3 * HALF] if second else [2 * HALF])
    count = 1 + len(others)
    W[:, 0:HALF] = pltpu.roll(T[pl.ds(r0, 32), own:own + HALF], lax.rem(HALF - shift, HALF), 1)
    for c, lane in enumerate(others):
        W[:, (c + 1) * HALF:(c + 2) * HALF] = T[pl.ds(r0, 32), lane:lane + HALF]
    for p in range(4):
        k0 = 8 * p
        cols = [
            jnp.broadcast_to(W[k0:32, k0 + m:k0 + m + 1], (32 - k0, HALF)) for m in range(8)
        ]
        e = {}
        for m in range(8):
            for i in range(m, 8):
                e[i, m] = jnp.broadcast_to(cols[m][i:i + 1, :], (8, HALF))
        r, l = {}, {}
        for j in range(8):
            r[j] = lax.rsqrt(e[j, j])
            for i in range(j + 1, 8):
                l[i, j] = e[i, j] * r[j]
            for k in range(j + 1, 8):
                for i in range(k, 8):
                    e[i, k] = e[i, k] - l[i, j] * l[k, j]
        rows = []
        for i in range(8):
            tiles = []
            for c in range(count):
                lanes = slice(c * HALF, (c + 1) * HALF)
                w = jnp.broadcast_to(W[k0 + i:k0 + i + 1, lanes], (8, HALF))
                for k in range(i):
                    w = w - l[i, k] * rows[k][c]
                tiles.append(w * r[i])
            rows.append(tiles)
        for t in range(1, 4 - p):
            lc = []
            for j in range(8):
                v = cols[j][8 * t:8 * t + 8, :]
                for k in range(j):
                    v = v - l[j, k] * lc[k]
                lc.append(v * r[j])
            for c in range(count):
                at = (slice(k0 + 8 * t, k0 + 8 * t + 8), slice(c * HALF, (c + 1) * HALF))
                w = W[at]
                for j in range(8):
                    w = w - lc[j] * rows[j][c]
                W[at] = w
        for i in range(8):
            for c in range(count):
                W[k0 + i:k0 + i + 1, c * HALF:(c + 1) * HALF] = rows[i][c][0:1, :]
    T[pl.ds(r0, 32), own:own + HALF] = pltpu.roll(W[:, 0:HALF], shift, 1)
    for c, lane in enumerate(others):
        T[pl.ds(r0, 32), lane:lane + HALF] = W[:, (c + 1) * HALF:(c + 2) * HALF]
    end = others[-1] + HALF if others else own + HALF
    a, b, c = split3(T[pl.ds(r0, 32), own:end])
    left = jnp.concatenate([a, a, b, b, a, c], axis=0)
    right = jnp.concatenate([a, b, a, b, c, a], axis=0)

    def update(first, lane):
        lo = lane - own
        product = dot(left[:, first - own:first - own + HALF], right[:, lo:], (0, 0))
        row = lax.broadcasted_iota(jnp.int32, product.shape, 0) + first
        T[first:first + HALF, lane:end] = (
            T[first:first + HALF, lane:end] - jnp.where(row >= r0 + 32, product, 0.0)
        )

    if second:
        @pl.when(s < 7)
        def _():
            update(HALF, HALF)
    else:
        @pl.when(s < 3)
        def _():
            update(0, 0)
        update(HALF, HALF)


def identity_matrix():
    i0 = lax.broadcasted_iota(jnp.int32, (RANK, RANK), 0)
    i1 = lax.broadcasted_iota(jnp.int32, (RANK, RANK), 1)
    return jnp.where(i0 == i1, 1.0, 0.0), i0 >= i1


def factor_capacitance(gram, rows, lower, T, W, hooks):
    identity, below = identity_matrix()
    T[:, 0:RANK] = identity + gram / rows
    T[:, RANK:2 * RANK] = identity

    def step(second, s, carry):
        for at, hook in hooks.items():
            if (at >= 4) == second:
                pl.when(s == at)(hook)
        super_panel(s, second, True, T, W)
        return carry

    lax.fori_loop(0, 4, functools.partial(step, False), 0)
    lax.fori_loop(4, 8, functools.partial(step, True), 0)
    lower[...] = jnp.where(below, T[:, 0:RANK].T, 0.0)
    return T[:, RANK:2 * RANK]


def send(src, dst, sems, at, peer):
    copy = pltpu.make_async_remote_copy(
        src_ref=src, dst_ref=dst, send_sem=sems.at[at], recv_sem=sems.at[at + 1],
        device_id=peer, device_id_type=MESH,
    )
    return copy


def drain(ref, sems, at):
    pltpu.make_async_copy(ref, ref, sems.at[at + 1]).wait()
    pltpu.make_async_copy(ref, ref, sems.at[at]).wait()


def chain_kernel(scale, node_rows, points, noise, landmarks, mixing,
                 bases, lower1, lower2, last,
                 cols, mix, V, VT, U, products, paired, total, landed, mine, full,
                 part, got, spare, T, W, sems, local):
    branch, row, chip, core = place()
    other = (branch, row + 1 - 2 * core)
    halves = ((branch ^ 16, row), (branch ^ 32, row))
    slab = pl.ds(pl.multiple_of(chip * SLAB, SLAB), SLAB)
    ids = (3 + branch // 16, 1 + branch // 32, 0)
    barrier = pltpu.get_barrier_semaphore()

    def loads(level):
        return pltpu.make_async_copy(mixing.at[ids[level]], mix.at[level], local.at[level])

    for level in range(3):
        loads(level).start()
    for peer in (other,) + halves:
        pl.semaphore_signal(barrier, inc=1, device_id=peer, device_id_type=MESH)

    def each_chip(action):
        def one(k, carry):
            action(k, chip ^ k)
            return carry
        lax.fori_loop(1, CHIPS, one, 0)

    each_chip(lambda k, peer: pl.semaphore_signal(
        barrier, inc=1, device_id=chip_id(branch, peer, core), device_id_type=MESH))

    def pair(batch):
        lo, hi = BATCHES[batch]
        return send(products.at[1 - core, lo:hi], paired.at[lo:hi], sems, 4 * batch, other)

    def scatter(batch):
        lo, hi = BATCHES[batch]
        pair(batch).wait()
        total[lo:hi] = products[core, lo:hi] + paired[lo:hi]

        def one(k, peer):
            rows = pl.ds(pl.multiple_of(peer * SLAB, SLAB), SLAB)
            send(total.at[lo:hi, rows, :], landed.at[k, lo:hi], sems, 4 * batch + 2,
                 chip_id(branch, peer, core)).start()
        each_chip(one)

    def collect(batch):
        lo, hi = BATCHES[batch]
        drain(landed.at[1:CHIPS, lo:hi], sems, 4 * batch + 2)
        value = total[lo:hi, slab, :]
        for k in range(1, CHIPS):
            value = value + landed[k, lo:hi]
        mine[lo:hi] = value

    def spread(g, ref):
        full[g, core, slab, :] = ref[...]
        each_chip(lambda k, peer: send(
            ref, full.at[g, core, slab, :], sems, 12 + 4 * g, chip_id(branch, peer, core)).start())

    def swap(g):
        return send(full.at[g, core], full.at[g, core], sems, 14 + 4 * g, other)

    def spread_done(g):
        drain(full.at[g, core, 0:RANK - SLAB, :], sems, 12 + 4 * g)
        swap(g).start()

    def match(at, lo, hi, peer):
        return send(part.at[lo:hi], got.at[lo:hi], sems, 36 + 2 * at, peer)

    def whole(g):
        return jnp.concatenate([full[g, 0], full[g, 1]], axis=1)

    def put(level):
        return pltpu.make_async_copy(V.at[level], bases.at[level], local.at[3 + level])

    chunks = V.shape[1] // CHUNK

    def loop(action):
        def one(i, carry):
            action(pl.ds(pl.multiple_of(i * CHUNK, CHUNK), CHUNK))
            return carry
        lax.fori_loop(0, chunks, one, 0)

    def unit(level):
        loads(level).wait()
        right = right3(split2(mix[level]))
        marks = [landmarks[pl.ds(ids[level], 1), c, :] for c in range(3)]

        def chunk(rows):
            spread_now = None
            for c in range(3):
                offset = cols[rows, c:c + 1] - marks[c]
                square = offset * offset
                spread_now = square if spread_now is None else spread_now + square
            kernel = jnp.exp(-spread_now * scale)
            value = dot(left3(split2(kernel), 1), right)
            weighted = value * (1.0 / cols[rows, 3:4])
            V[level, rows, :] = weighted
            for n, piece in enumerate(split2(value)):
                U[n, rows, :] = piece
            for n, piece in enumerate(split2(weighted)):
                VT[level, n, :, rows] = piece.T
        loop(chunk)

    def multiply(batch):
        lo, hi = BATCHES[batch]
        products[:, lo:hi] = jnp.zeros((2, hi - lo, RANK, HALF), f32)

        def chunk(rows):
            right = right3((U[0, rows, :], U[1, rows, :]))
            for b in range(lo, hi):
                i = BLOCKS[b][0]
                product = dot(left3((VT[i, 0, :, rows], VT[i, 1, :, rows]), 1), right)
                products[0, b] += product[:, :HALF]
                products[1, b] += product[:, HALF:]
        loop(chunk)

    cols[...] = jnp.concatenate(
        [points[...], noise[...], jnp.zeros((4, V.shape[1]), f32)], axis=0).T
    unit(0)
    multiply(0)
    pl.semaphore_wait(barrier, 3 + CHIPS - 1)
    pair(0).start()
    put(0).start()
    unit(1)
    scatter(0)
    multiply(1)
    pair(1).start()
    unit(2)
    collect(0)
    spread(0, mine.at[0])
    scatter(1)
    multiply(2)
    pair(2).start()
    spread_done(0)
    swap(0).wait()

    def late_scatter():
        scatter(2)

    def second_cross():
        collect(1)
        spread(1, mine.at[1])

    def third_cross():
        spread_done(1)
        collect(2)
        spread(2, mine.at[3])

    def minus(value, left, right, rows):
        product = mm(left, right, (0, 0)) / rows
        spare[0] = product[:, :HALF]
        spare[1] = product[:, HALF:]
        return value - spare[core, slab, :]

    inverse = factor_capacitance(
        whole(0), node_rows, lower1, T, W, {0: late_scatter, 2: second_cross, 6: third_cross})
    swap(1).wait()
    y12 = mm(inverse, whole(1))
    part[0] = minus(mine[2], y12, y12, node_rows)
    match(0, 0, 1, halves[0]).start()
    c12 = right3(split2(mm(inverse, y12, (0, 0)) / node_rows))

    match(0, 0, 1, halves[0]).wait()
    mine[0] = part[0] + got[0]
    spread(3, mine.at[0])
    spread_done(2)
    swap(2).wait()
    y13 = mm(inverse, whole(2))
    part[1] = minus(mine[4], y12, y13, node_rows)
    part[2] = minus(mine[5], y13, y13, node_rows)
    match(1, 1, 3, halves[0]).start()
    c13 = right3(split2(mm(inverse, y13, (0, 0)) / node_rows))
    spread_done(3)

    def second(rows):
        left = left3(split2(V[0, rows, :]), 1)
        V[1, rows, :] = V[1, rows, :] - dot(left, c12)
        V[2, rows, :] = V[2, rows, :] - dot(left, c13)
    loop(second)
    put(1).start()
    swap(3).wait()

    def cross_match():
        match(1, 1, 3, halves[0]).wait()
        mine[1:3] = part[1:3] + got[1:3]
        spread(4, mine.at[1])

    def cross_swap():
        spread_done(4)

    inverse = factor_capacitance(
        whole(3), 2.0 * node_rows, lower2, T, W, {1: cross_match, 6: cross_swap})
    swap(4).wait()
    y23 = mm(inverse, whole(4))
    part[3] = minus(mine[2], y23, y23, 2.0 * node_rows)
    match(2, 3, 4, halves[1]).start()
    c23 = right3(split2(mm(inverse, y23, (0, 0)) / (2.0 * node_rows)))
    match(2, 3, 4, halves[1]).wait()
    mine[3] = part[3] + got[3]
    spread(5, mine.at[3])

    def third(rows):
        V[2, rows, :] = V[2, rows, :] - dot(left3(split2(V[1, rows, :]), 1), c23)
    loop(third)
    put(2).start()
    spread_done(5)
    swap(5).wait()
    last[...] = full[5]
    for level in range(3):
        put(level).wait()


def chain(points, noise, landmarks, mixing, node_rows):
    rows = points.shape[1]
    length_scale = 0.6 * RANK ** (-1.0 / 3.0)
    scale = 1.0 / (2.0 * length_scale * length_scale)
    vmem = pl.BlockSpec(memory_space=pltpu.VMEM)
    hbm = pl.BlockSpec(memory_space=pl.ANY)
    square = jax.ShapeDtypeStruct((RANK, RANK), f32)
    return pl.pallas_call(
        functools.partial(chain_kernel, scale, node_rows),
        in_specs=[vmem, vmem, vmem, hbm],
        out_specs=[hbm, vmem, vmem, vmem],
        out_shape=[
            jax.ShapeDtypeStruct((3, rows, RANK), f32), square, square,
            jax.ShapeDtypeStruct((2, RANK, HALF), f32),
        ],
        scratch_shapes=[
            pltpu.VMEM((rows, 8), f32),
            pltpu.VMEM((3, RANK, RANK), f32),
            pltpu.VMEM((3, rows, RANK), f32),
            pltpu.VMEM((3, 2, RANK, rows), bf16),
            pltpu.VMEM((2, rows, RANK), bf16),
            pltpu.VMEM((2, 6, RANK, HALF), f32),
            pltpu.VMEM((6, RANK, HALF), f32),
            pltpu.VMEM((6, RANK, HALF), f32),
            pltpu.VMEM((CHIPS, 6, SLAB, HALF), f32),
            pltpu.VMEM((6, SLAB, HALF), f32),
            pltpu.VMEM((6, 2, RANK, HALF), f32),
            pltpu.VMEM((4, SLAB, HALF), f32),
            pltpu.VMEM((4, SLAB, HALF), f32),
            pltpu.VMEM((2, RANK, HALF), f32),
            pltpu.VMEM((RANK, 2 * RANK), f32),
            pltpu.VMEM((32, 4 * HALF), f32),
            pltpu.SemaphoreType.DMA((42,)),
            pltpu.SemaphoreType.DMA((6,)),
        ],
        compiler_params=pltpu.CompilerParams(
            collective_id=0, has_side_effects=True, vmem_limit_bytes=48 * 1024 * 1024),
        name="chain",
    )(points, noise[None], landmarks, mixing)


def finish_kernel(rows, solved, lower1, lower2, gram, bases, factors, T, W):
    s = pl.program_id(0)
    bases[...] = solved[...]

    @pl.when(s == 0)
    def _():
        T[...] = identity_matrix()[0] + jnp.concatenate([gram[0], gram[1]], axis=1) / rows
        factors[0, 0] = lower1[...]
        factors[0, 1] = lower2[...]

    @pl.when(s < 4)
    def _():
        super_panel(s, False, False, T, W)

    @pl.when(s >= 4)
    def _():
        super_panel(s, True, False, T, W)

    @pl.when(s == 7)
    def _():
        factors[0, 2] = jnp.where(identity_matrix()[1], T[...].T, 0.0)


def finish(solved, lower1, lower2, gram, rows):
    square = pl.BlockSpec((RANK, RANK), lambda i: (0, 0))
    block = pl.BlockSpec((3, solved.shape[1] // 8, RANK), lambda i: (0, i, 0))
    return pl.pallas_call(
        functools.partial(finish_kernel, rows),
        grid=(8,),
        in_specs=[block, square, square, pl.BlockSpec((2, RANK, HALF), lambda i: (0, 0, 0))],
        out_specs=[block, pl.BlockSpec((1, 3, RANK, RANK), lambda i: (0, 0, 0, 0))],
        out_shape=[
            jax.ShapeDtypeStruct(solved.shape, f32),
            jax.ShapeDtypeStruct((1, 3, RANK, RANK), f32),
        ],
        scratch_shapes=[pltpu.VMEM((RANK, RANK), f32), pltpu.VMEM((32, 2 * HALF), f32)],
        name="finish",
    )(solved, lower1, lower2, gram)


def on_device(points, noise, landmarks, mixing):
    node_rows = float(NODE_BRANCHES * lax.axis_size("rows") * points.shape[1])
    solved, lower1, lower2, gram = chain(points, noise, landmarks, mixing, node_rows)
    return tuple(finish(solved, lower1, lower2, gram, 4.0 * node_rows))


def solution(mesh):
    in_specs = (P(None, ("branch", "rows")), P(("branch", "rows")), P(), P())
    out_specs = (P(None, ("branch", "rows"), None), P("branch", None, None, None))
    return jax.shard_map(
        on_device, mesh=mesh, in_specs=in_specs, out_specs=out_specs, check_vma=False
    )
```

time: 538 us -> 98.6 us (0.18)
  the two profiles are of different devices: /device:TPU:8 before, /device:TPU:1 now
where the time goes in v2:
time: 98.6 us; the launch traced here: 98.2 us
  Pallas kernels  91.7 us (93%)
  local copies, waits for them, and re-layouts  5.81 us (6%)
    pallas_call x1, Pallas kernels, chain(): pl.pallas_call(functools.partial(chain_kernel, scale, node_rows), in_spec...  78.2 us
    pallas_call x1, Pallas kernels, finish(): pl.pallas_call(functools.partial(finish_kernel, rows), grid=(8,), in_spec...  13.5 us
    unnamed x13, local copies, waits for them, and re-layouts  5.81 us

profile of v2, /device:TPU:1, one launch (start us, length us, event | category | flops | bytes accessed | tf_op | source)
XLA Modules:
  0.0 98.2 jit_solution(18037414635298917685)
XLA Ops:
  0.6 0.8 copy.6.landmarks
  1.4 0.0 copy-start
  1.4 1.5 %copy-done = f32[7,256,256]{2,1,0:T(8,128)S(1)} copy-done((f32[7,256,256]{2,1,0:T(8,128)S(1)}, f32[7,256,256]{2,1,0:T(8,128)}, u32[]{:S(2)}) %copy-start) | copy-done | bytes 1835032
  2.9 0.0 copy-start.4
  2.9 0.8 copy-done.4
  3.6 0.0 copy-start.5
  3.6 0.7 copy-done.5
  4.3 78.2 %chain.1 = (f32[3,2048,256]{2,1,0:T(8,128)}, f32[256,256]{1,0:T(8,128)S(1)}, f32[256,256]{1,0:T(8,128)S(1)}, f32[2,256,128]{2,1,0:T(8,128)S(1)}) custom-call(f32[3,2048]{1,0:T(4,128)S(1)} %copy-done.4, f32[1,2048]{1,0:T(1,128)S(1)} %bitcast.1, f32[7,3,256]{2,1,0:T(4,128)S(1)} %copy.6.landmarks, f32[7,256,256]{2,1,0:T(8,128)S(1)} %copy-done), custom_call_target="tpu_custom_call" | custom-call | tf_op jit(solution)/shard_map/chain/pallas_call | solution.py:404
  82.5 0.0 copy-start.1
  82.6 0.7 copy-done.1
  83.2 0.0 copy-start.2
  83.2 0.7 copy-done.2
  84.0 0.0 copy-start.3
  84.0 0.7 copy-done.3
  84.7 13.5 %finish.1 = (f32[3,2048,256]{2,1,0:T(8,128)}, f32[1,3,256,256]{3,2,1,0:T(8,128)}) custom-call(f32[3,2048,256]{2,1,0:T(8,128)} %get-tuple-element.6.solved, f32[256,256]{1,0:T(8,128)} %copy-done.1, f32[256,256]{1,0:T(8,128)} %copy-done.2, f32[2,256,128]{2,1,0:T(8,128)} %copy-done.3), custom_call_target="tpu_custom_call" | custom-call | tf_op jit(solution)/shard_map/finish/pallas_call | solution.py:464
Async XLA Ops:
  1.4 1.5 %copy-start = (f32[7,256,256]{2,1,0:T(8,128)S(1)}, f32[7,256,256]{2,1,0:T(8,128)}, u32[]{:S(2)}) copy-start(f32[7,256,256]{2,1,0:T(8,128)} %mixing.1) | copy-start | bytes 5505028
  2.9 0.8 copy-start.4
  3.6 0.7 copy-start.5
  82.5 0.7 copy-start.1
  83.2 0.7 copy-start.2
  84.0 0.7 copy-start.3

commit v3 on v2

--- a/solution.py
+++ b/solution.py
@@ -18,6 +18,7 @@
 NODE_BRANCHES = 16
 CHUNK = 512
 BLOCKS = ((0, 0), (0, 1), (1, 1), (0, 2), (1, 2), (2, 2))
+FACTOR_SCRATCH = (pltpu.VMEM((32, 32, HALF), f32), pltpu.VMEM((8, 32, HALF), f32))
 BATCHES = ((0, 1), (1, 3), (3, 6))
 
 
@@ -66,7 +67,7 @@
     )
 
 
-def super_panel(s, second, wide, T, W):
+def super_panel(s, second, wide, T, W, C, M):
     r0 = pl.multiple_of(s * 32, 32)
     shift = lax.rem(s, 4) * 32
     own = HALF if second else 0
@@ -74,18 +75,20 @@
     if wide:
         others = others + ([2 * HALF, 3 * HALF] if second else [2 * HALF])
     count = 1 + len(others)
-    W[:, 0:HALF] = pltpu.roll(T[pl.ds(r0, 32), own:own + HALF], lax.rem(HALF - shift, HALF), 1)
-    for c, lane in enumerate(others):
-        W[:, (c + 1) * HALF:(c + 2) * HALF] = T[pl.ds(r0, 32), lane:lane + HALF]
+    lanes_of = [own] + others
+    for c, lane in enumerate(lanes_of):
+        W[:, c * HALF:(c + 1) * HALF] = T[pl.ds(r0, 32), lane:lane + HALF]
+    square = W[:, 0:HALF]
+    for q in range(4):
+        for m in range(8):
+            C[8 * q + m, 8 * q:32] = jnp.take_along_axis(
+                square[8 * q:32], jnp.full((32 - 8 * q, HALF), shift + 8 * q + m, jnp.int32), axis=1)
     for p in range(4):
         k0 = 8 * p
-        cols = [
-            jnp.broadcast_to(W[k0:32, k0 + m:k0 + m + 1], (32 - k0, HALF)) for m in range(8)
-        ]
         e = {}
         for m in range(8):
             for i in range(m, 8):
-                e[i, m] = jnp.broadcast_to(cols[m][i:i + 1, :], (8, HALF))
+                e[i, m] = jnp.broadcast_to(C[k0 + m, k0 + i:k0 + i + 1, :], (8, HALF))
         r, l = {}, {}
         for j in range(8):
             r[j] = lax.rsqrt(e[j, j])
@@ -94,6 +97,25 @@
             for k in range(j + 1, 8):
                 for i in range(k, 8):
                     e[i, k] = e[i, k] - l[i, j] * l[k, j]
+        lower = {}
+        for t in range(p + 1, 4):
+            for j in range(8):
+                v = C[k0 + j, 8 * t:8 * t + 8, :]
+                for k in range(j):
+                    v = v - l[j, k] * lower[t, k]
+                lower[t, j] = v * r[j]
+                M[j, 8 * t:8 * t + 8, :] = lower[t, j]
+        for q in range(p + 1, 4):
+            for m in range(8):
+                across = [
+                    jnp.broadcast_to(M[j, 8 * q + m:8 * q + m + 1, :], (8, HALF)) for j in range(8)
+                ]
+                for t in range(q, 4):
+                    at = (8 * q + m, slice(8 * t, 8 * t + 8))
+                    v = C[at]
+                    for j in range(8):
+                        v = v - lower[t, j] * across[j]
+                    C[at] = v
         rows = []
         for i in range(8):
             tiles = []
@@ -104,25 +126,18 @@
                     w = w - l[i, k] * rows[k][c]
                 tiles.append(w * r[i])
             rows.append(tiles)
-        for t in range(1, 4 - p):
-            lc = []
-            for j in range(8):
-                v = cols[j][8 * t:8 * t + 8, :]
-                for k in range(j):
-                    v = v - l[j, k] * lc[k]
-                lc.append(v * r[j])
+        for t in range(p + 1, 4):
             for c in range(count):
-                at = (slice(k0 + 8 * t, k0 + 8 * t + 8), slice(c * HALF, (c + 1) * HALF))
+                at = (slice(8 * t, 8 * t + 8), slice(c * HALF, (c + 1) * HALF))
                 w = W[at]
                 for j in range(8):
-                    w = w - lc[j] * rows[j][c]
+                    w = w - lower[t, j] * rows[j][c]
                 W[at] = w
         for i in range(8):
             for c in range(count):
                 W[k0 + i:k0 + i + 1, c * HALF:(c + 1) * HALF] = rows[i][c][0:1, :]
-    T[pl.ds(r0, 32), own:own + HALF] = pltpu.roll(W[:, 0:HALF], shift, 1)
-    for c, lane in enumerate(others):
-        T[pl.ds(r0, 32), lane:lane + HALF] = W[:, (c + 1) * HALF:(c + 2) * HALF]
+    for c, lane in enumerate(lanes_of):
+        T[pl.ds(r0, 32), lane:lane + HALF] = W[:, c * HALF:(c + 1) * HALF]
     end = others[-1] + HALF if others else own + HALF
     a, b, c = split3(T[pl.ds(r0, 32), own:end])
     left = jnp.concatenate([a, a, b, b, a, c], axis=0)
@@ -153,7 +168,7 @@
     return jnp.where(i0 == i1, 1.0, 0.0), i0 >= i1
 
 
-def factor_capacitance(gram, rows, lower, T, W, hooks):
+def factor_capacitance(gram, rows, lower, T, W, C, M, hooks):
     identity, below = identity_matrix()
     T[:, 0:RANK] = identity + gram / rows
     T[:, RANK:2 * RANK] = identity
@@ -162,7 +177,7 @@
         for at, hook in hooks.items():
             if (at >= 4) == second:
                 pl.when(s == at)(hook)
-        super_panel(s, second, True, T, W)
+        super_panel(s, second, True, T, W, C, M)
         return carry
 
     lax.fori_loop(0, 4, functools.partial(step, False), 0)
@@ -185,9 +200,9 @@
 
 
 def chain_kernel(scale, node_rows, points, noise, landmarks, mixing,
-                 bases, lower1, lower2, last,
-                 cols, mix, V, VT, U, products, paired, total, landed, mine, full,
-                 part, got, spare, T, W, sems, local):
+                 bases, lower1_out, lower2_out, last_out,
+                 points_in, noise_in, marks_in, lower1, lower2, cols, mix, V, VT, U, products, paired, total, landed, mine, full,
+                 part, got, spare, T, W, C, M, sems, local):
     branch, row, chip, core = place()
     other = (branch, row + 1 - 2 * core)
     halves = ((branch ^ 16, row), (branch ^ 32, row))
@@ -198,6 +213,12 @@
     def loads(level):
         return pltpu.make_async_copy(mixing.at[ids[level]], mix.at[level], local.at[level])
 
+    inputs = [
+        pltpu.make_async_copy(src, dst, local.at[6 + n]) for n, (src, dst) in enumerate(
+            ((points, points_in), (noise, noise_in), (landmarks, marks_in)))
+    ]
+    for copy in inputs:
+        copy.start()
     for level in range(3):
         loads(level).start()
     for peer in (other,) + halves:
@@ -267,7 +288,7 @@
     def unit(level):
         loads(level).wait()
         right = right3(split2(mix[level]))
-        marks = [landmarks[pl.ds(ids[level], 1), c, :] for c in range(3)]
+        marks = [marks_in[c, pl.ds(ids[level], 1), :] for c in range(3)]
 
         def chunk(rows):
             spread_now = None
@@ -298,8 +319,10 @@
                 products[1, b] += product[:, HALF:]
         loop(chunk)
 
+    for copy in inputs:
+        copy.wait()
     cols[...] = jnp.concatenate(
-        [points[...], noise[...], jnp.zeros((4, V.shape[1]), f32)], axis=0).T
+        [points_in[...], noise_in[...], jnp.zeros((4, V.shape[1]), f32)], axis=0).T
     unit(0)
     multiply(0)
     pl.semaphore_wait(barrier, 3 + CHIPS - 1)
@@ -337,7 +360,9 @@
         return value - spare[core, slab, :]
 
     inverse = factor_capacitance(
-        whole(0), node_rows, lower1, T, W, {0: late_scatter, 2: second_cross, 6: third_cross})
+        whole(0), node_rows, lower1, T, W, C, M, {0: late_scatter, 2: second_cross, 6: third_cross})
+    put_lower1 = pltpu.make_async_copy(lower1, lower1_out, local.at[9])
+    put_lower1.start()
     swap(1).wait()
     y12 = mm(inverse, whole(1))
     part[0] = minus(mine[2], y12, y12, node_rows)
@@ -373,7 +398,9 @@
         spread_done(4)
 
     inverse = factor_capacitance(
-        whole(3), 2.0 * node_rows, lower2, T, W, {1: cross_match, 6: cross_swap})
+        whole(3), 2.0 * node_rows, lower2, T, W, C, M, {1: cross_match, 6: cross_swap})
+    put_lower2 = pltpu.make_async_copy(lower2, lower2_out, local.at[10])
+    put_lower2.start()
     swap(4).wait()
     y23 = mm(inverse, whole(4))
     part[3] = minus(mine[2], y23, y23, 2.0 * node_rows)
@@ -389,27 +416,35 @@
     put(2).start()
     spread_done(5)
     swap(5).wait()
-    last[...] = full[5]
+    put_last = pltpu.make_async_copy(full.at[5], last_out, local.at[11])
+    put_last.start()
     for level in range(3):
         put(level).wait()
+    put_lower1.wait()
+    put_lower2.wait()
+    put_last.wait()
 
 
 def chain(points, noise, landmarks, mixing, node_rows):
     rows = points.shape[1]
     length_scale = 0.6 * RANK ** (-1.0 / 3.0)
     scale = 1.0 / (2.0 * length_scale * length_scale)
-    vmem = pl.BlockSpec(memory_space=pltpu.VMEM)
     hbm = pl.BlockSpec(memory_space=pl.ANY)
     square = jax.ShapeDtypeStruct((RANK, RANK), f32)
     return pl.pallas_call(
         functools.partial(chain_kernel, scale, node_rows),
-        in_specs=[vmem, vmem, vmem, hbm],
-        out_specs=[hbm, vmem, vmem, vmem],
+        in_specs=[hbm] * 4,
+        out_specs=[hbm] * 4,
         out_shape=[
             jax.ShapeDtypeStruct((3, rows, RANK), f32), square, square,
             jax.ShapeDtypeStruct((2, RANK, HALF), f32),
         ],
         scratch_shapes=[
+            pltpu.VMEM((3, rows), f32),
+            pltpu.VMEM((1, rows), f32),
+            pltpu.VMEM((3, 7, RANK), f32),
+            pltpu.VMEM((RANK, RANK), f32),
+            pltpu.VMEM((RANK, RANK), f32),
             pltpu.VMEM((rows, 8), f32),
             pltpu.VMEM((3, RANK, RANK), f32),
             pltpu.VMEM((3, rows, RANK), f32),
@@ -426,16 +461,17 @@
             pltpu.VMEM((2, RANK, HALF), f32),
             pltpu.VMEM((RANK, 2 * RANK), f32),
             pltpu.VMEM((32, 4 * HALF), f32),
+            pltpu.VMEM((32, 32, HALF), f32), pltpu.VMEM((8, 32, HALF), f32),
             pltpu.SemaphoreType.DMA((42,)),
-            pltpu.SemaphoreType.DMA((6,)),
+            pltpu.SemaphoreType.DMA((12,)),
         ],
         compiler_params=pltpu.CompilerParams(
-            collective_id=0, has_side_effects=True, vmem_limit_bytes=48 * 1024 * 1024),
+            collective_id=0, has_side_effects=True),
         name="chain",
-    )(points, noise[None], landmarks, mixing)
-
-
-def finish_kernel(rows, solved, lower1, lower2, gram, bases, factors, T, W):
+    )(points, noise[None], jnp.transpose(landmarks, (1, 0, 2)), mixing)
+
+
+def finish_kernel(rows, solved, lower1, lower2, gram, bases, factors, T, W, C, M):
     s = pl.program_id(0)
     bases[...] = solved[...]
 
@@ -447,11 +483,11 @@
 
     @pl.when(s < 4)
     def _():
-        super_panel(s, False, False, T, W)
+        super_panel(s, False, False, T, W, C, M)
 
     @pl.when(s >= 4)
     def _():
-        super_panel(s, True, False, T, W)
+        super_panel(s, True, False, T, W, C, M)
 
     @pl.when(s == 7)
     def _():
@@ -470,7 +506,10 @@
             jax.ShapeDtypeStruct(solved.shape, f32),
             jax.ShapeDtypeStruct((1, 3, RANK, RANK), f32),
         ],
-        scratch_shapes=[pltpu.VMEM((RANK, RANK), f32), pltpu.VMEM((32, 2 * HALF), f32)],
+        scratch_shapes=[
+            pltpu.VMEM((RANK, RANK), f32), pltpu.VMEM((32, 2 * HALF), f32),
+            pltpu.VMEM((32, 32, HALF), f32), pltpu.VMEM((8, 32, HALF), f32),
+        ],
         name="finish",
     )(solved, lower1, lower2, gram)
 

time: 98.6 us -> 89.7 us (0.910)
  local copies, waits for them, and re-layouts: 5.81 us -> 0 us
  Pallas kernels: 91.7 us -> 88.7 us
    unnamed x13 -> x0, local copies, waits for them, and re-layouts: 5.81 us -> none
    pallas_call x1, Pallas kernels: 13.5 us -> 11.9 us  [finish(): pl.pallas_call(functools.partial(finish_kernel, rows), grid=(8,), in_spec...]
    pallas_call x1, Pallas kernels: 78.2 us -> 76.8 us  [chain(): pl.pallas_call(functools.partial(chain_kernel, scale, node_rows), in_spec...]
where the time goes in v3:
time: 89.7 us; the launch traced here: 89.3 us
  Pallas kernels  88.7 us (99%)
    pallas_call x1, Pallas kernels, chain(): pl.pallas_call(functools.partial(chain_kernel, scale, node_rows), in_spec...  76.8 us
    pallas_call x1, Pallas kernels, finish(): pl.pallas_call(functools.partial(finish_kernel, rows), grid=(8,), in_spec...  11.9 us

profile of v3, /device:TPU:1, one launch (start us, length us, event | category | flops | bytes accessed | tf_op | source)
XLA Modules:
  0.0 89.3 jit_solution(4153316618888270847)
XLA Ops:
  0.6 76.8 %chain.1 = (f32[3,2048,256]{2,1,0:T(8,128)}, f32[256,256]{1,0:T(8,128)}, f32[256,256]{1,0:T(8,128)}, f32[2,256,128]{2,1,0:T(8,128)}) custom-call(f32[3,2048]{1,0:T(4,128)} %points.1, f32[1,2048]{1,0:T(1,128)} %bitcast.3, f32[3,7,256]{2,1,0:T(8,128)} %bitcast.2, f32[7,256,256]{2,1,0:T(8,128)} %mixing.1), custom_call_target="tpu_custom_call" | custom-call | tf_op jit(solution)/shard_map/chain/pallas_call | solution.py:434
  77.4 11.9 %finish.1 = (f32[3,2048,256]{2,1,0:T(8,128)}, f32[1,3,256,256]{3,2,1,0:T(8,128)}) custom-call(f32[3,2048,256]{2,1,0:T(8,128)} %get-tuple-element.6.solved, f32[256,256]{1,0:T(8,128)} %get-tuple-element.7.lower1, f32[256,256]{1,0:T(8,128)} %get-tuple-element.8.lower2, f32[2,256,128]{2,1,0:T(8,128)} %get-tuple-element.9.gram), custom_call_target="tpu_custom_call" | custom-call | tf_op jit(solution)/shard_map/finish/pallas_call | solution.py:500
